TPU v7x, 512 devices: a whole 4x8x8 slice. The times are simulated.
512 devices in a mesh: band: 4 (over x), tile: 16 (over y_lo, z), slab: 8 (over y_hi, core).
Axes of the slice: x: 4, y: 8 (y_hi: 4, y_lo: 2; y = y_hi * 2 + y_lo), z: 8, core: 2. Of those that a mesh axis runs over, the one named last changes fastest.
Arguments:
- strength: float32 [32], P('band'), may hold values from 0.0005 to 0.5
- opacity: float32 [64, 256, 256], P('slab', 'tile'), may hold values from 0.5 to 2
- planck: float32 [64, 256, 256], P('slab', 'tile'), may hold values from 0.5 to 2
- old_populations: float32 [5, 64, 256, 256], P(None, 'slab', 'tile'), may hold values from 0.1 to 1
- line_index: int32 [32], P('band'), may hold values from 0 to 4
- line_weight: float32 [32], P('band'), may hold values from 0.2 to 1
Outputs:
- new_populations: float32 [5, 64, 256, 256], P(None, 'slab', 'tile', 'band')
- new_source: float32 [32, 64, 256, 256], P('band', 'slab', 'tile')
Inputs may be any that keep to these rules, and one draw needn't show every extreme that they name: line_index names a transition of the model atom.
All inputs are finite; a program needn't handle non-finite values.
Results may differ from a plain program's by a relative error of at most 0.0001.
Values sent between devices are 32-bit elements; how exact they have to be, the bound alone decides.
No kernel may reach another device: no remote copies, remote signals or barrier semaphores. Data moves between devices by JAX's collectives and lax.ppermute only.
A program may use at most 64 MiB of HBM per device.

v0:
```python
import jax
import jax.numpy as jnp
from jax import lax
from jax.sharding import PartitionSpec as P

LINES = 5
EPS_THERMAL = 0.1
COLLISION = 0.5
PATH_FACTOR = 1.25
TILT_SHARE = 0.4
LOWER_LEVEL = (0, 0, 1, 1, 2)
UPPER_LEVEL = (3, 4, 3, 4, 4)


def extended_2(cells, sides, width):
    for axis, dim in sides:
        count = lax.axis_size(axis)
        ends = count - 1
        head = lax.slice_in_dim(cells, 0, width, axis=dim)
        tail = lax.slice_in_dim(cells, cells.shape[dim] - width, cells.shape[dim], axis=dim)
        cells = jnp.concatenate(
            [
                lax.ppermute(tail, axis, [(i, (i + 1) % count) for i in range(ends)]),
                cells,
                lax.ppermute(head, axis, [((i + 1) % count, i) for i in range(ends)]),
            ],
            axis=dim,
        )
    return cells


def shifted(block, axis, distance):
    devices = range(lax.axis_size(axis))
    route = [(i - distance, i) for i in devices if i - distance in devices]
    return lax.ppermute(block, axis, route)


def relax(jbar, planck):
    ratios = (jbar + COLLISION * planck[None]) / (1.0 + jbar + COLLISION)
    ground = jnp.ones_like(planck)
    level_three = ratios[0]
    level_four = ratios[1]
    level_one = 0.5 * (level_three / ratios[2] + level_four / ratios[3])
    level_two = level_four / ratios[4]
    stacked = jnp.stack([ground, level_one, level_two, level_three, level_four], axis=0)
    return stacked / jnp.sum(stacked, axis=0)


def line_sources(levels_now):
    return jnp.stack(
        [
            levels_now[UPPER_LEVEL[t]] / (levels_now[LOWER_LEVEL[t]] + levels_now[UPPER_LEVEL[t]])
            for t in range(5)
        ],
        axis=0,
    )


def sweep(face_ext, strength, opacity_ext, source_ext, margin):
    intensity = face_ext
    layer_sums = []
    for plane in range(opacity_ext.shape[0]):
        attenuation = jnp.exp(-PATH_FACTOR * strength[:, None, None] * opacity_ext[plane][None])[
            :, None
        ]
        zero_column = jnp.zeros_like(intensity[:, 0, :1])
        from_left = jnp.concatenate([zero_column, intensity[:, 0, :-1]], axis=1)
        from_right = jnp.concatenate([intensity[:, 1, 1:], zero_column], axis=1)
        upwind = jnp.stack([from_left, from_right], axis=1)
        intensity = (
            attenuation * ((1.0 - TILT_SHARE) * intensity + TILT_SHARE * upwind)
            + (1.0 - attenuation) * source_ext[:, plane][:, None]
        )
        layer_sums.append(jnp.sum(intensity[:, :, margin:-margin], axis=1))
    return (intensity[:, :, margin:-margin], jnp.stack(layer_sums, axis=1))


def per_device(strength, opacity, planck, old_populations, line_index, line_weight):
    highest = lax.Precision.HIGHEST
    slab_depth, tile_rows, cells_y = opacity.shape
    freq_count = strength.shape[0]
    total_freqs = freq_count * lax.axis_size("band")
    onehot = (line_index[:, None] == jnp.arange(LINES, dtype=jnp.int32)[None, :]).astype(
        jnp.float32
    )
    weighted = onehot * line_weight[:, None] * (LINES / (2.0 * total_freqs))
    fields = jnp.concatenate([opacity[None], planck[None], old_populations], axis=0)
    fields_ext = extended_2(fields, (("tile", 2),), slab_depth)
    opacity_ext = fields_ext[0]
    planck_ext = fields_ext[1]
    levels_ext = fields_ext[2:]
    extended = tile_rows + 2 * slab_depth
    global_x = (
        lax.axis_index("tile") * tile_rows - slab_depth + jnp.arange(extended, dtype=jnp.int32)
    )
    inside = ((global_x >= 0) & (global_x < tile_rows * lax.axis_size("tile")))[None, :, None]
    lower_ext = jnp.stack([levels_ext[LOWER_LEVEL[t]] for t in range(5)], axis=0)
    upper_ext = jnp.stack([levels_ext[UPPER_LEVEL[t]] for t in range(5)], axis=0)
    denominator = jnp.where(inside, lower_ext + upper_ext, 1.0)
    line_ext = jnp.where(inside, upper_ext / denominator, 0.0)
    source_ext = jnp.where(
        inside,
        EPS_THERMAL * planck_ext[None]
        + (1.0 - EPS_THERMAL) * jnp.einsum("ft,tzxy->fzxy", onehot, line_ext, precision=highest),
        0.0,
    )
    slab_count = lax.axis_size("slab")

    def whole_step(step, carry):
        face_in, previous = carry
        face_ext = extended_2(face_in, (("tile", 2),), slab_depth)
        bottom, layer_sums = sweep(face_ext, strength, opacity_ext, source_ext, slab_depth)
        return (shifted(bottom, "slab", 1), layer_sums)

    face_start = jnp.zeros((freq_count, 2, tile_rows, cells_y), jnp.float32)
    initial = (face_start, jnp.zeros((freq_count, slab_depth, tile_rows, cells_y), jnp.float32))
    _, layer_sums = lax.fori_loop(0, slab_count, whole_step, initial)
    jbar = jnp.einsum("ft,fzxy->tzxy", weighted, layer_sums, precision=highest)
    share = cells_y // lax.axis_size("band")
    offset = lax.axis_index("band") * share
    jbar_share = lax.psum_scatter(jbar, "band", scatter_dimension=3, tiled=True)
    planck_share = lax.dynamic_slice_in_dim(planck, offset, share, 2)
    populations_share = relax(jbar_share, planck_share)
    populations_all = lax.all_gather(populations_share, "band", axis=3, tiled=True)
    new_source = EPS_THERMAL * planck[None] + (1.0 - EPS_THERMAL) * jnp.einsum(
        "ft,tzxy->fzxy", onehot, line_sources(populations_all), precision=highest
    )
    return (populations_share, new_source)


def solution(mesh):
    in_specs = (
        P("band"),
        P("slab", "tile", None),
        P("slab", "tile", None),
        P(None, "slab", "tile", None),
        P("band"),
        P("band"),
    )
    out_specs = (P(None, "slab", "tile", "band"), P("band", "slab", "tile", None))
    return jax.shard_map(
        per_device, mesh=mesh, in_specs=in_specs, out_specs=out_specs, check_vma=False
    )
```

profile of v0, /device:TPU:8, one launch (start us, length us, event | category | flops | bytes accessed | tf_op | source)
XLA Modules:
  0.0 435.0 jit_solution(6454355539191148617)
XLA Ops:
  8.7 4.3 collective-permute-start.3
  13.0 8.5 %collective-permute-start.4 = (f32[7,8,8,256]{3,2,1,0:T(8,128)S(1)}, f32[7,8,8,256]{3,2,1,0:T(8,128)}, u32[]{:S(2)}, u32[]{:S(2)}) collective-permute-start(f32[7,8,8,256]{3,2,1,0:T(8,128)S(1)} %get-tuple-element.113), channel_id=1, source_target_pairs={{8,0},{16,8},{24,16},{32,24},{40,32},{48,40},{56,48},{64,56},{72,6... | collective-permute-start | bytes 1376264 | tf_op jit(solution)/shard_map/ppermute | solution.py:25
  21.5 8.5 %collective-permute-done.3 = f32[7,8,8,256]{3,2,1,0:T(8,128)S(1)} collective-permute-done((f32[7,8,8,256]{3,2,1,0:T(8,128)S(1)}, f32[7,8,8,256]{3,2,1,0:T(8,128)S(1)}, u32[]{:S(2)}, u32[]{:S(2)}) %collective-permute-start.3) | collective-permute-done | bytes 458784 | tf_op jit(solution)/shard_map/ppermute | solution.py:23
  37.6 251.7 %while.12 = (s32[]{:T(128)}, f32[8,2,16,256]{3,2,0,1:T(8,128)S(1)}, f32[8,8,16,256]{3,2,0,1:T(8,128)}, f32[8]{0:T(128)S(1)}, f32[8,32,256]{2,1,0:T(8,128)S(1)}, /*index=5*/f32[8,8,32,256]{3,2,0,1:T(8,128)}, s32[]{:T(128)}) while((s32[]{:T(128)}, f32[8,2,16,256]{3,2,0,1:T(8,128)S(1)}, f32[8,8,16,256]{3,2,0,1:T(8,128)}, f32[8]{0:T(128)S(1)}, ...), condition=%wide.region_9.10_spmd, body=%wide.region_0.9_spmd.sunk | while | flops 24772616 | bytes 81658408 | solution.py:117
  40.5 6.6 %collective-permute-start.1 = (f32[8,2,8,256]{3,2,0,1:T(8,128)}, f32[8,2,8,256]{3,2,0,1:T(8,128)}, u32[]{:S(2)}, u32[]{:S(2)}) collective-permute-start(f32[8,2,8,256]{3,2,0,1:T(8,128)} %get-tuple-element.218), channel_id=1, source_target_pairs={{8,0},{16,8},{24,16},{32,24},{40,32},{48,40},{56,48},{64,56},{72,6... | collective-permute-start | bytes 393224 | tf_op jit(solution)/shard_map/while/body/eval_jaxpr/ppermute | solution.py:25
  67.0 6.0 %collective-permute-start.1 = (f32[8,2,8,256]{3,2,0,1:T(8,128)}, f32[8,2,8,256]{3,2,0,1:T(8,128)}, u32[]{:S(2)}, u32[]{:S(2)}) collective-permute-start(f32[8,2,8,256]{3,2,0,1:T(8,128)} %get-tuple-element.218), channel_id=1, source_target_pairs={{8,0},{16,8},{24,16},{32,24},{40,32},{48,40},{56,48},{64,56},{72,6... | collective-permute-start | bytes 393224 | tf_op jit(solution)/shard_map/while/body/eval_jaxpr/ppermute | solution.py:25
  87.8 6.8 %collective-permute-start.2 = (f32[8,2,16,256]{3,2,0,1:T(8,128)S(1)}, f32[8,2,16,256]{3,2,0,1:T(8,128)S(1)}, u32[]{:S(2)}, u32[]{:S(2)}) collective-permute-start(f32[8,2,16,256]{3,2,0,1:T(8,128)S(1)} %get-tuple-element.252), channel_id=1, source_target_pairs={{0,1},{1,2},{2,3},{3,4},{4,5},{5,6},{6,7},{8,9},{9,10},{10,11},{11... | collective-permute-start | bytes 786440 | tf_op jit(solution)/shard_map/while/body/eval_jaxpr/ppermute | solution.py:35
  98.5 6.0 %collective-permute-start.1 = (f32[8,2,8,256]{3,2,0,1:T(8,128)}, f32[8,2,8,256]{3,2,0,1:T(8,128)}, u32[]{:S(2)}, u32[]{:S(2)}) collective-permute-start(f32[8,2,8,256]{3,2,0,1:T(8,128)} %get-tuple-element.218), channel_id=1, source_target_pairs={{8,0},{16,8},{24,16},{32,24},{40,32},{48,40},{56,48},{64,56},{72,6... | collective-permute-start | bytes 393224 | tf_op jit(solution)/shard_map/while/body/eval_jaxpr/ppermute | solution.py:25
  119.3 7.5 %collective-permute-start.2 = (f32[8,2,16,256]{3,2,0,1:T(8,128)S(1)}, f32[8,2,16,256]{3,2,0,1:T(8,128)S(1)}, u32[]{:S(2)}, u32[]{:S(2)}) collective-permute-start(f32[8,2,16,256]{3,2,0,1:T(8,128)S(1)} %get-tuple-element.252), channel_id=1, source_target_pairs={{0,1},{1,2},{2,3},{3,4},{4,5},{5,6},{6,7},{8,9},{9,10},{10,11},{11... | collective-permute-start | bytes 786440 | tf_op jit(solution)/shard_map/while/body/eval_jaxpr/ppermute | solution.py:35
  130.7 6.0 %collective-permute-start.1 = (f32[8,2,8,256]{3,2,0,1:T(8,128)}, f32[8,2,8,256]{3,2,0,1:T(8,128)}, u32[]{:S(2)}, u32[]{:S(2)}) collective-permute-start(f32[8,2,8,256]{3,2,0,1:T(8,128)} %get-tuple-element.218), channel_id=1, source_target_pairs={{8,0},{16,8},{24,16},{32,24},{40,32},{48,40},{56,48},{64,56},{72,6... | collective-permute-start | bytes 393224 | tf_op jit(solution)/shard_map/while/body/eval_jaxpr/ppermute | solution.py:25
  151.5 7.6 %collective-permute-start.2 = (f32[8,2,16,256]{3,2,0,1:T(8,128)S(1)}, f32[8,2,16,256]{3,2,0,1:T(8,128)S(1)}, u32[]{:S(2)}, u32[]{:S(2)}) collective-permute-start(f32[8,2,16,256]{3,2,0,1:T(8,128)S(1)} %get-tuple-element.252), channel_id=1, source_target_pairs={{0,1},{1,2},{2,3},{3,4},{4,5},{5,6},{6,7},{8,9},{9,10},{10,11},{11... | collective-permute-start | bytes 786440 | tf_op jit(solution)/shard_map/while/body/eval_jaxpr/ppermute | solution.py:35
  162.9 6.0 %collective-permute-start.1 = (f32[8,2,8,256]{3,2,0,1:T(8,128)}, f32[8,2,8,256]{3,2,0,1:T(8,128)}, u32[]{:S(2)}, u32[]{:S(2)}) collective-permute-start(f32[8,2,8,256]{3,2,0,1:T(8,128)} %get-tuple-element.218), channel_id=1, source_target_pairs={{8,0},{16,8},{24,16},{32,24},{40,32},{48,40},{56,48},{64,56},{72,6... | collective-permute-start | bytes 393224 | tf_op jit(solution)/shard_map/while/body/eval_jaxpr/ppermute | solution.py:25
  183.7 7.6 %collective-permute-start.2 = (f32[8,2,16,256]{3,2,0,1:T(8,128)S(1)}, f32[8,2,16,256]{3,2,0,1:T(8,128)S(1)}, u32[]{:S(2)}, u32[]{:S(2)}) collective-permute-start(f32[8,2,16,256]{3,2,0,1:T(8,128)S(1)} %get-tuple-element.252), channel_id=1, source_target_pairs={{0,1},{1,2},{2,3},{3,4},{4,5},{5,6},{6,7},{8,9},{9,10},{10,11},{11... | collective-permute-start | bytes 786440 | tf_op jit(solution)/shard_map/while/body/eval_jaxpr/ppermute | solution.py:35
  195.1 6.0 %collective-permute-start.1 = (f32[8,2,8,256]{3,2,0,1:T(8,128)}, f32[8,2,8,256]{3,2,0,1:T(8,128)}, u32[]{:S(2)}, u32[]{:S(2)}) collective-permute-start(f32[8,2,8,256]{3,2,0,1:T(8,128)} %get-tuple-element.218), channel_id=1, source_target_pairs={{8,0},{16,8},{24,16},{32,24},{40,32},{48,40},{56,48},{64,56},{72,6... | collective-permute-start | bytes 393224 | tf_op jit(solution)/shard_map/while/body/eval_jaxpr/ppermute | solution.py:25
  215.9 7.6 %collective-permute-start.2 = (f32[8,2,16,256]{3,2,0,1:T(8,128)S(1)}, f32[8,2,16,256]{3,2,0,1:T(8,128)S(1)}, u32[]{:S(2)}, u32[]{:S(2)}) collective-permute-start(f32[8,2,16,256]{3,2,0,1:T(8,128)S(1)} %get-tuple-element.252), channel_id=1, source_target_pairs={{0,1},{1,2},{2,3},{3,4},{4,5},{5,6},{6,7},{8,9},{9,10},{10,11},{11... | collective-permute-start | bytes 786440 | tf_op jit(solution)/shard_map/while/body/eval_jaxpr/ppermute | solution.py:35
  227.3 6.0 %collective-permute-start.1 = (f32[8,2,8,256]{3,2,0,1:T(8,128)}, f32[8,2,8,256]{3,2,0,1:T(8,128)}, u32[]{:S(2)}, u32[]{:S(2)}) collective-permute-start(f32[8,2,8,256]{3,2,0,1:T(8,128)} %get-tuple-element.218), channel_id=1, source_target_pairs={{8,0},{16,8},{24,16},{32,24},{40,32},{48,40},{56,48},{64,56},{72,6... | collective-permute-start | bytes 393224 | tf_op jit(solution)/shard_map/while/body/eval_jaxpr/ppermute | solution.py:25
  248.1 7.6 %collective-permute-start.2 = (f32[8,2,16,256]{3,2,0,1:T(8,128)S(1)}, f32[8,2,16,256]{3,2,0,1:T(8,128)S(1)}, u32[]{:S(2)}, u32[]{:S(2)}) collective-permute-start(f32[8,2,16,256]{3,2,0,1:T(8,128)S(1)} %get-tuple-element.252), channel_id=1, source_target_pairs={{0,1},{1,2},{2,3},{3,4},{4,5},{5,6},{6,7},{8,9},{9,10},{10,11},{11... | collective-permute-start | bytes 786440 | tf_op jit(solution)/shard_map/while/body/eval_jaxpr/ppermute | solution.py:35
  259.5 6.0 %collective-permute-start.1 = (f32[8,2,8,256]{3,2,0,1:T(8,128)}, f32[8,2,8,256]{3,2,0,1:T(8,128)}, u32[]{:S(2)}, u32[]{:S(2)}) collective-permute-start(f32[8,2,8,256]{3,2,0,1:T(8,128)} %get-tuple-element.218), channel_id=1, source_target_pairs={{8,0},{16,8},{24,16},{32,24},{40,32},{48,40},{56,48},{64,56},{72,6... | collective-permute-start | bytes 393224 | tf_op jit(solution)/shard_map/while/body/eval_jaxpr/ppermute | solution.py:25
  280.3 7.8 %collective-permute-start.2 = (f32[8,2,16,256]{3,2,0,1:T(8,128)S(1)}, f32[8,2,16,256]{3,2,0,1:T(8,128)S(1)}, u32[]{:S(2)}, u32[]{:S(2)}) collective-permute-start(f32[8,2,16,256]{3,2,0,1:T(8,128)S(1)} %get-tuple-element.252), channel_id=1, source_target_pairs={{0,1},{1,2},{2,3},{3,4},{4,5},{5,6},{6,7},{8,9},{9,10},{10,11},{11... | collective-permute-start | bytes 786440 | tf_op jit(solution)/shard_map/while/body/eval_jaxpr/ppermute | solution.py:35
  292.1 13.8 %copy.27 = f32[5,8,16,256]{0,2,1,3:T(8,128)} copy(f32[5,8,16,256]{3,0,2,1:T(8,128)S(1)} %fusion.33) | data formatting | bytes 1310720
  305.9 11.9 %reshape.106 = f32[256,640]{1,0:T(8,128)} reshape(f32[256,8,16,5]{3,2,1,0:T(8,128)} %bitcast.211) | data formatting | bytes 1310720
  318.6 43.0 %reduce-scatter.4.cloned.1.call-done = f32[64,640]{1,0:T(8,128)} async-done(((f32[256,640]{1,0:T(8,128)}), f32[64,640]{1,0:T(8,128)}) %reduce-scatter.4.cloned.1.call-update) | async-done | bytes 163856
  361.5 6.2 %reshape.107 = f32[64,8,16,5]{3,2,1,0:T(8,128)} reshape(f32[64,640]{1,0:T(8,128)} %reduce-scatter.4.cloned.1.call-done) | data formatting | bytes 327680
  373.9 45.2 %all_gather.3 = f32[5,8,16,256]{2,1,0,3:T(8,128)S(1)} all-gather(f32[5,8,16,64]{2,1,0,3:T(8,128)S(1)} %copy.14), channel_id=1, replica_groups=mesh['band'=4,'tile'=16,'slab'=8] {'band'}, dimensions={3}, use_global_device_ids=true | all-gather | bytes 819200 | tf_op jit(solution)/shard_map/all_gather | solution.py:124
  (654 shorter events, 174.3 us)
Async XLA Ops:
  7.2 354.4 %reduce-scatter.4.cloned.1.call-start = ((), (), s32[]{:S(2)}) async-start(), calls=%async_computation.1 | async-start | bytes 819200
  8.7 21.3 %collective-permute-start.3 = (f32[7,8,8,256]{3,2,1,0:T(8,128)S(1)}, f32[7,8,8,256]{3,2,1,0:T(8,128)S(1)}, u32[]{:S(2)}, u32[]{:S(2)}) collective-permute-start(f32[7,8,8,256]{3,2,1,0:T(8,128)S(1)} %get-tuple-element.112), channel_id=1, source_target_pairs={{0,8},{8,16},{16,24},{24,32},{32,40},{40,48},{48,56},{56,64},{64,7... | collective-permute-start | bytes 1376264 | tf_op jit(solution)/shard_map/ppermute | solution.py:23
  13.0 18.2 %collective-permute-start.4 = (f32[7,8,8,256]{3,2,1,0:T(8,128)S(1)}, f32[7,8,8,256]{3,2,1,0:T(8,128)}, u32[]{:S(2)}, u32[]{:S(2)}) collective-permute-start(f32[7,8,8,256]{3,2,1,0:T(8,128)S(1)} %get-tuple-element.113), channel_id=1, source_target_pairs={{8,0},{16,8},{24,16},{32,24},{40,32},{48,40},{56,48},{64,56},{72,6... | collective-permute-start | bytes 1376264 | tf_op jit(solution)/shard_map/ppermute | solution.py:25
  38.6 13.2 %collective-permute-start = (f32[8,2,8,256]{3,2,0,1:T(8,128)}, f32[8,2,8,256]{3,2,0,1:T(8,128)}, u32[]{:S(2)}, u32[]{:S(2)}) collective-permute-start(f32[8,2,8,256]{3,2,0,1:T(8,128)} %get-tuple-element.217), channel_id=1, source_target_pairs={{0,8},{8,16},{16,24},{24,32},{32,40},{40,48},{48,56},{56,64},{64,7... | collective-permute-start | bytes 393224 | tf_op jit(solution)/shard_map/while/body/eval_jaxpr/ppermute | solution.py:23
  40.5 13.1 %collective-permute-start.1 = (f32[8,2,8,256]{3,2,0,1:T(8,128)}, f32[8,2,8,256]{3,2,0,1:T(8,128)}, u32[]{:S(2)}, u32[]{:S(2)}) collective-permute-start(f32[8,2,8,256]{3,2,0,1:T(8,128)} %get-tuple-element.218), channel_id=1, source_target_pairs={{8,0},{16,8},{24,16},{32,24},{40,32},{48,40},{56,48},{64,56},{72,6... | collective-permute-start | bytes 393224 | tf_op jit(solution)/shard_map/while/body/eval_jaxpr/ppermute | solution.py:25
  65.1 12.6 %collective-permute-start = (f32[8,2,8,256]{3,2,0,1:T(8,128)}, f32[8,2,8,256]{3,2,0,1:T(8,128)}, u32[]{:S(2)}, u32[]{:S(2)}) collective-permute-start(f32[8,2,8,256]{3,2,0,1:T(8,128)} %get-tuple-element.217), channel_id=1, source_target_pairs={{0,8},{8,16},{16,24},{24,32},{32,40},{40,48},{48,56},{56,64},{64,7... | collective-permute-start | bytes 393224 | tf_op jit(solution)/shard_map/while/body/eval_jaxpr/ppermute | solution.py:23
  67.0 12.6 %collective-permute-start.1 = (f32[8,2,8,256]{3,2,0,1:T(8,128)}, f32[8,2,8,256]{3,2,0,1:T(8,128)}, u32[]{:S(2)}, u32[]{:S(2)}) collective-permute-start(f32[8,2,8,256]{3,2,0,1:T(8,128)} %get-tuple-element.218), channel_id=1, source_target_pairs={{8,0},{16,8},{24,16},{32,24},{40,32},{48,40},{56,48},{64,56},{72,6... | collective-permute-start | bytes 393224 | tf_op jit(solution)/shard_map/while/body/eval_jaxpr/ppermute | solution.py:25
  96.6 12.6 %collective-permute-start = (f32[8,2,8,256]{3,2,0,1:T(8,128)}, f32[8,2,8,256]{3,2,0,1:T(8,128)}, u32[]{:S(2)}, u32[]{:S(2)}) collective-permute-start(f32[8,2,8,256]{3,2,0,1:T(8,128)} %get-tuple-element.217), channel_id=1, source_target_pairs={{0,8},{8,16},{16,24},{24,32},{32,40},{40,48},{48,56},{56,64},{64,7... | collective-permute-start | bytes 393224 | tf_op jit(solution)/shard_map/while/body/eval_jaxpr/ppermute | solution.py:23
  98.5 12.6 %collective-permute-start.1 = (f32[8,2,8,256]{3,2,0,1:T(8,128)}, f32[8,2,8,256]{3,2,0,1:T(8,128)}, u32[]{:S(2)}, u32[]{:S(2)}) collective-permute-start(f32[8,2,8,256]{3,2,0,1:T(8,128)} %get-tuple-element.218), channel_id=1, source_target_pairs={{8,0},{16,8},{24,16},{32,24},{40,32},{48,40},{56,48},{64,56},{72,6... | collective-permute-start | bytes 393224 | tf_op jit(solution)/shard_map/while/body/eval_jaxpr/ppermute | solution.py:25
  128.7 12.6 %collective-permute-start = (f32[8,2,8,256]{3,2,0,1:T(8,128)}, f32[8,2,8,256]{3,2,0,1:T(8,128)}, u32[]{:S(2)}, u32[]{:S(2)}) collective-permute-start(f32[8,2,8,256]{3,2,0,1:T(8,128)} %get-tuple-element.217), channel_id=1, source_target_pairs={{0,8},{8,16},{16,24},{24,32},{32,40},{40,48},{48,56},{56,64},{64,7... | collective-permute-start | bytes 393224 | tf_op jit(solution)/shard_map/while/body/eval_jaxpr/ppermute | solution.py:23
  130.7 12.6 %collective-permute-start.1 = (f32[8,2,8,256]{3,2,0,1:T(8,128)}, f32[8,2,8,256]{3,2,0,1:T(8,128)}, u32[]{:S(2)}, u32[]{:S(2)}) collective-permute-start(f32[8,2,8,256]{3,2,0,1:T(8,128)} %get-tuple-element.218), channel_id=1, source_target_pairs={{8,0},{16,8},{24,16},{32,24},{40,32},{48,40},{56,48},{64,56},{72,6... | collective-permute-start | bytes 393224 | tf_op jit(solution)/shard_map/while/body/eval_jaxpr/ppermute | solution.py:25
  151.5 8.7 %collective-permute-start.2 = (f32[8,2,16,256]{3,2,0,1:T(8,128)S(1)}, f32[8,2,16,256]{3,2,0,1:T(8,128)S(1)}, u32[]{:S(2)}, u32[]{:S(2)}) collective-permute-start(f32[8,2,16,256]{3,2,0,1:T(8,128)S(1)} %get-tuple-element.252), channel_id=1, source_target_pairs={{0,1},{1,2},{2,3},{3,4},{4,5},{5,6},{6,7},{8,9},{9,10},{10,11},{11... | collective-permute-start | bytes 786440 | tf_op jit(solution)/shard_map/while/body/eval_jaxpr/ppermute | solution.py:35
  160.9 12.6 %collective-permute-start = (f32[8,2,8,256]{3,2,0,1:T(8,128)}, f32[8,2,8,256]{3,2,0,1:T(8,128)}, u32[]{:S(2)}, u32[]{:S(2)}) collective-permute-start(f32[8,2,8,256]{3,2,0,1:T(8,128)} %get-tuple-element.217), channel_id=1, source_target_pairs={{0,8},{8,16},{16,24},{24,32},{32,40},{40,48},{48,56},{56,64},{64,7... | collective-permute-start | bytes 393224 | tf_op jit(solution)/shard_map/while/body/eval_jaxpr/ppermute | solution.py:23
  162.9 12.6 %collective-permute-start.1 = (f32[8,2,8,256]{3,2,0,1:T(8,128)}, f32[8,2,8,256]{3,2,0,1:T(8,128)}, u32[]{:S(2)}, u32[]{:S(2)}) collective-permute-start(f32[8,2,8,256]{3,2,0,1:T(8,128)} %get-tuple-element.218), channel_id=1, source_target_pairs={{8,0},{16,8},{24,16},{32,24},{40,32},{48,40},{56,48},{64,56},{72,6... | collective-permute-start | bytes 393224 | tf_op jit(solution)/shard_map/while/body/eval_jaxpr/ppermute | solution.py:25
  183.7 8.7 %collective-permute-start.2 = (f32[8,2,16,256]{3,2,0,1:T(8,128)S(1)}, f32[8,2,16,256]{3,2,0,1:T(8,128)S(1)}, u32[]{:S(2)}, u32[]{:S(2)}) collective-permute-start(f32[8,2,16,256]{3,2,0,1:T(8,128)S(1)} %get-tuple-element.252), channel_id=1, source_target_pairs={{0,1},{1,2},{2,3},{3,4},{4,5},{5,6},{6,7},{8,9},{9,10},{10,11},{11... | collective-permute-start | bytes 786440 | tf_op jit(solution)/shard_map/while/body/eval_jaxpr/ppermute | solution.py:35
  193.2 12.6 %collective-permute-start = (f32[8,2,8,256]{3,2,0,1:T(8,128)}, f32[8,2,8,256]{3,2,0,1:T(8,128)}, u32[]{:S(2)}, u32[]{:S(2)}) collective-permute-start(f32[8,2,8,256]{3,2,0,1:T(8,128)} %get-tuple-element.217), channel_id=1, source_target_pairs={{0,8},{8,16},{16,24},{24,32},{32,40},{40,48},{48,56},{56,64},{64,7... | collective-permute-start | bytes 393224 | tf_op jit(solution)/shard_map/while/body/eval_jaxpr/ppermute | solution.py:23
  195.1 12.6 %collective-permute-start.1 = (f32[8,2,8,256]{3,2,0,1:T(8,128)}, f32[8,2,8,256]{3,2,0,1:T(8,128)}, u32[]{:S(2)}, u32[]{:S(2)}) collective-permute-start(f32[8,2,8,256]{3,2,0,1:T(8,128)} %get-tuple-element.218), channel_id=1, source_target_pairs={{8,0},{16,8},{24,16},{32,24},{40,32},{48,40},{56,48},{64,56},{72,6... | collective-permute-start | bytes 393224 | tf_op jit(solution)/shard_map/while/body/eval_jaxpr/ppermute | solution.py:25
  215.9 8.7 %collective-permute-start.2 = (f32[8,2,16,256]{3,2,0,1:T(8,128)S(1)}, f32[8,2,16,256]{3,2,0,1:T(8,128)S(1)}, u32[]{:S(2)}, u32[]{:S(2)}) collective-permute-start(f32[8,2,16,256]{3,2,0,1:T(8,128)S(1)} %get-tuple-element.252), channel_id=1, source_target_pairs={{0,1},{1,2},{2,3},{3,4},{4,5},{5,6},{6,7},{8,9},{9,10},{10,11},{11... | collective-permute-start | bytes 786440 | tf_op jit(solution)/shard_map/while/body/eval_jaxpr/ppermute | solution.py:35
  225.4 12.6 %collective-permute-start = (f32[8,2,8,256]{3,2,0,1:T(8,128)}, f32[8,2,8,256]{3,2,0,1:T(8,128)}, u32[]{:S(2)}, u32[]{:S(2)}) collective-permute-start(f32[8,2,8,256]{3,2,0,1:T(8,128)} %get-tuple-element.217), channel_id=1, source_target_pairs={{0,8},{8,16},{16,24},{24,32},{32,40},{40,48},{48,56},{56,64},{64,7... | collective-permute-start | bytes 393224 | tf_op jit(solution)/shard_map/while/body/eval_jaxpr/ppermute | solution.py:23
  227.3 12.6 %collective-permute-start.1 = (f32[8,2,8,256]{3,2,0,1:T(8,128)}, f32[8,2,8,256]{3,2,0,1:T(8,128)}, u32[]{:S(2)}, u32[]{:S(2)}) collective-permute-start(f32[8,2,8,256]{3,2,0,1:T(8,128)} %get-tuple-element.218), channel_id=1, source_target_pairs={{8,0},{16,8},{24,16},{32,24},{40,32},{48,40},{56,48},{64,56},{72,6... | collective-permute-start | bytes 393224 | tf_op jit(solution)/shard_map/while/body/eval_jaxpr/ppermute | solution.py:25
  248.1 8.7 %collective-permute-start.2 = (f32[8,2,16,256]{3,2,0,1:T(8,128)S(1)}, f32[8,2,16,256]{3,2,0,1:T(8,128)S(1)}, u32[]{:S(2)}, u32[]{:S(2)}) collective-permute-start(f32[8,2,16,256]{3,2,0,1:T(8,128)S(1)} %get-tuple-element.252), channel_id=1, source_target_pairs={{0,1},{1,2},{2,3},{3,4},{4,5},{5,6},{6,7},{8,9},{9,10},{10,11},{11... | collective-permute-start | bytes 786440 | tf_op jit(solution)/shard_map/while/body/eval_jaxpr/ppermute | solution.py:35
  257.6 12.6 %collective-permute-start = (f32[8,2,8,256]{3,2,0,1:T(8,128)}, f32[8,2,8,256]{3,2,0,1:T(8,128)}, u32[]{:S(2)}, u32[]{:S(2)}) collective-permute-start(f32[8,2,8,256]{3,2,0,1:T(8,128)} %get-tuple-element.217), channel_id=1, source_target_pairs={{0,8},{8,16},{16,24},{24,32},{32,40},{40,48},{48,56},{56,64},{64,7... | collective-permute-start | bytes 393224 | tf_op jit(solution)/shard_map/while/body/eval_jaxpr/ppermute | solution.py:23
  259.5 12.6 %collective-permute-start.1 = (f32[8,2,8,256]{3,2,0,1:T(8,128)}, f32[8,2,8,256]{3,2,0,1:T(8,128)}, u32[]{:S(2)}, u32[]{:S(2)}) collective-permute-start(f32[8,2,8,256]{3,2,0,1:T(8,128)} %get-tuple-element.218), channel_id=1, source_target_pairs={{8,0},{16,8},{24,16},{32,24},{40,32},{48,40},{56,48},{64,56},{72,6... | collective-permute-start | bytes 393224 | tf_op jit(solution)/shard_map/while/body/eval_jaxpr/ppermute | solution.py:25
  280.3 9.0 %collective-permute-start.2 = (f32[8,2,16,256]{3,2,0,1:T(8,128)S(1)}, f32[8,2,16,256]{3,2,0,1:T(8,128)S(1)}, u32[]{:S(2)}, u32[]{:S(2)}) collective-permute-start(f32[8,2,16,256]{3,2,0,1:T(8,128)S(1)} %get-tuple-element.252), channel_id=1, source_target_pairs={{0,1},{1,2},{2,3},{3,4},{4,5},{5,6},{6,7},{8,9},{9,10},{10,11},{11... | collective-permute-start | bytes 786440 | tf_op jit(solution)/shard_map/while/body/eval_jaxpr/ppermute | solution.py:35
  (76 other events, 603.8 us)
Sparse Core Ops, SparseCore 0:
  317.9 43.5 reduce-scatter.3
where the time goes:
time: 438 us; the launch traced here: 435 us
  starting transfers between devices  131 us (30%)
  local copies, waits for them, and re-layouts  107 us (24%)
  other arithmetic  69.3 us (16%)
  waiting for transfers between devices  59.8 us (14%)
  blocking collectives  45.2 us (10%)
  between operations  14.3 us (3%)
  matrix products  5.26 us (1%)
    ppermute x9, starting transfers between devices, extended_2(): lax.ppermute(head, axis, [((i + 1) % count, i) for i in range(ends)])  57.3 us
    ppermute x8, starting transfers between devices, shifted(): return lax.ppermute(block, axis, route)  53.7 us
    add x64, other arithmetic, sweep(): attenuation * ((1.0 - TILT_SHARE) * intensity + TILT_SHARE * upwind)  51.4 us
    all_gather x1, blocking collectives, per_device(): lax.all_gather(populations_share, 'band', axis=3, tiled=True)  45.2 us
    unnamed x29, local copies, waits for them, and re-layouts  43.1 us
    unnamed x2, waiting for transfers between devices  43 us
    while x200, local copies, waits for them, and re-layouts  35.4 us
    ppermute x9, starting transfers between devices, extended_2(): lax.ppermute(tail, axis, [(i, (i + 1) % count) for i in range(ends)])  19.6 us
  transfers between devices with their start and end apart: 27, of which 11 were waited for; matrix products, arithmetic and copies ran while one was open for 12% of the time, Pallas kernels for 0%

commit v1 on v0

--- a/solution.py
+++ b/solution.py
@@ -121,7 +121,18 @@
     jbar_share = lax.psum_scatter(jbar, "band", scatter_dimension=3, tiled=True)
     planck_share = lax.dynamic_slice_in_dim(planck, offset, share, 2)
     populations_share = relax(jbar_share, planck_share)
-    populations_all = lax.all_gather(populations_share, "band", axis=3, tiled=True)
+    size_here = lax.axis_size("band")
+    buffer = [(to_i, (to_i + 1) % size_here) for to_i in range(size_here)]
+    b_now, y2 = ([populations_share], [populations_share])
+    row_list = [(to_i, (to_i - 1) % size_here) for to_i in range(size_here)]
+    for _ in range(size_here // 2):
+        b_now.append(lax.ppermute(b_now[-1], "band", buffer))
+    for _ in range((size_here - 1) // 2):
+        y2.append(lax.ppermute(y2[-1], perm=row_list, axis_name="band"))
+    later = jnp.concatenate([*b_now[::-1], *y2[1:]], 3)
+    populations_all = jnp.roll(
+        later, (lax.axis_index("band") - size_here // 2) * populations_share.shape[3], 3
+    )
     new_source = EPS_THERMAL * planck[None] + (1.0 - EPS_THERMAL) * jnp.einsum(
         "ft,tzxy->fzxy", onehot, line_sources(populations_all), precision=highest
     )

time: 438 us -> 420 us (0.959)
  blocking collectives: 45.2 us -> 0 us
  waiting for transfers between devices: 59.8 us -> 80.2 us
  starting transfers between devices: 131 us -> 140 us
    all_gather x1 -> x0, blocking collectives: 45.2 us -> none  [per_device(): lax.all_gather(populations_share, 'band', axis=3, tiled=True)]
    ppermute x0 -> x3, waiting for transfers between devices: none -> 19.7 us  [the longest x2 19.7 us: per_device(): b_now.append(lax.ppermute(b_now[-1], 'band', buffer))]
    ppermute x0 -> x3, starting transfers between devices: none -> 8.96 us  [the longest x1 5.13 us: per_device(): y2.append(lax.ppermute(y2[-1], perm=row_list, axis_name='band'))]
    unnamed x29 -> x24, local copies, waits for them, and re-layouts: 43.1 us -> 39.6 us
  transfers between devices with their start and end apart: 27 -> 30, of which waited for: 11 -> 13; matrix products, arithmetic and copies ran while one was open for 12% -> 13% of each run, Pallas kernels for 0% -> 0%
where the time goes in v1:
time: 420 us; the launch traced here: 418 us
  starting transfers between devices  140 us (33%)
  local copies, waits for them, and re-layouts  104 us (25%)
  waiting for transfers between devices  80.2 us (19%)
  other arithmetic  70 us (17%)
  between operations  14.3 us (3%)
  matrix products  5.26 us (1%)
    ppermute x9, starting transfers between devices, extended_2(): lax.ppermute(head, axis, [((i + 1) % count, i) for i in range(ends)])  57.3 us
    ppermute x8, starting transfers between devices, shifted(): return lax.ppermute(block, axis, route)  53.8 us
    add x64, other arithmetic, sweep(): attenuation * ((1.0 - TILT_SHARE) * intensity + TILT_SHARE * upwind)  51.4 us
    unnamed x2, waiting for transfers between devices  43.7 us
    unnamed x24, local copies, waits for them, and re-layouts  39.6 us
    while x200, local copies, waits for them, and re-layouts  35.4 us
    ppermute x2, waiting for transfers between devices, per_device(): b_now.append(lax.ppermute(b_now[-1], 'band', buffer))  19.7 us
    ppermute x9, starting transfers between devices, extended_2(): lax.ppermute(tail, axis, [(i, (i + 1) % count) for i in range(ends)])  19.6 us
  transfers between devices with their start and end apart: 30, of which 13 were waited for; matrix products, arithmetic and copies ran while one was open for 13% of the time, Pallas kernels for 0%

profile of v1, /device:TPU:8, one launch (start us, length us, event | category | flops | bytes accessed | tf_op | source)
XLA Modules:
  0.0 417.7 jit_solution(6495448627549572889)
XLA Ops:
  13.0 8.5 %collective-permute-start.4 = (f32[7,8,8,256]{3,2,1,0:T(8,128)S(1)}, f32[7,8,8,256]{3,2,1,0:T(8,128)}, u32[]{:S(2)}, u32[]{:S(2)}) collective-permute-start(f32[7,8,8,256]{3,2,1,0:T(8,128)S(1)} %get-tuple-element.113), channel_id=1, source_target_pairs={{8,0},{16,8},{24,16},{32,24},{40,32},{48,40},{56,48},{64,56},{72,6... | collective-permute-start | bytes 1376264 | tf_op jit(solution)/shard_map/ppermute | solution.py:25
  21.5 8.5 %collective-permute-done.3 = f32[7,8,8,256]{3,2,1,0:T(8,128)S(1)} collective-permute-done((f32[7,8,8,256]{3,2,1,0:T(8,128)S(1)}, f32[7,8,8,256]{3,2,1,0:T(8,128)S(1)}, u32[]{:S(2)}, u32[]{:S(2)}) %collective-permute-start.3) | collective-permute-done | bytes 458784 | tf_op jit(solution)/shard_map/ppermute | solution.py:23
  37.6 252.0 %while.12 = (s32[]{:T(128)}, f32[8,2,16,256]{3,2,0,1:T(8,128)S(1)}, f32[8,8,16,256]{3,2,0,1:T(8,128)}, f32[8]{0:T(128)S(1)}, f32[8,32,256]{2,1,0:T(8,128)S(1)}, /*index=5*/f32[8,8,32,256]{3,2,0,1:T(8,128)}, s32[]{:T(128)}) while((s32[]{:T(128)}, f32[8,2,16,256]{3,2,0,1:T(8,128)S(1)}, f32[8,8,16,256]{3,2,0,1:T(8,128)}, f32[8]{0:T(128)S(1)}, ...), condition=%wide.region_9.10_spmd, body=%wide.region_0.9_spmd.sunk | while | flops 24772616 | bytes 81658408 | solution.py:117
  40.5 6.6 %collective-permute-start.1 = (f32[8,2,8,256]{3,2,0,1:T(8,128)}, f32[8,2,8,256]{3,2,0,1:T(8,128)}, u32[]{:S(2)}, u32[]{:S(2)}) collective-permute-start(f32[8,2,8,256]{3,2,0,1:T(8,128)} %get-tuple-element.208), channel_id=1, source_target_pairs={{8,0},{16,8},{24,16},{32,24},{40,32},{48,40},{56,48},{64,56},{72,6... | collective-permute-start | bytes 393224 | tf_op jit(solution)/shard_map/while/body/eval_jaxpr/ppermute | solution.py:25
  67.1 6.0 %collective-permute-start.1 = (f32[8,2,8,256]{3,2,0,1:T(8,128)}, f32[8,2,8,256]{3,2,0,1:T(8,128)}, u32[]{:S(2)}, u32[]{:S(2)}) collective-permute-start(f32[8,2,8,256]{3,2,0,1:T(8,128)} %get-tuple-element.208), channel_id=1, source_target_pairs={{8,0},{16,8},{24,16},{32,24},{40,32},{48,40},{56,48},{64,56},{72,6... | collective-permute-start | bytes 393224 | tf_op jit(solution)/shard_map/while/body/eval_jaxpr/ppermute | solution.py:25
  87.9 6.8 %collective-permute-start.2 = (f32[8,2,16,256]{3,2,0,1:T(8,128)S(1)}, f32[8,2,16,256]{3,2,0,1:T(8,128)S(1)}, u32[]{:S(2)}, u32[]{:S(2)}) collective-permute-start(f32[8,2,16,256]{3,2,0,1:T(8,128)S(1)} %get-tuple-element.242), channel_id=1, source_target_pairs={{0,1},{1,2},{2,3},{3,4},{4,5},{5,6},{6,7},{8,9},{9,10},{10,11},{11... | collective-permute-start | bytes 786440 | tf_op jit(solution)/shard_map/while/body/eval_jaxpr/ppermute | solution.py:35
  98.6 6.0 %collective-permute-start.1 = (f32[8,2,8,256]{3,2,0,1:T(8,128)}, f32[8,2,8,256]{3,2,0,1:T(8,128)}, u32[]{:S(2)}, u32[]{:S(2)}) collective-permute-start(f32[8,2,8,256]{3,2,0,1:T(8,128)} %get-tuple-element.208), channel_id=1, source_target_pairs={{8,0},{16,8},{24,16},{32,24},{40,32},{48,40},{56,48},{64,56},{72,6... | collective-permute-start | bytes 393224 | tf_op jit(solution)/shard_map/while/body/eval_jaxpr/ppermute | solution.py:25
  119.4 7.5 %collective-permute-start.2 = (f32[8,2,16,256]{3,2,0,1:T(8,128)S(1)}, f32[8,2,16,256]{3,2,0,1:T(8,128)S(1)}, u32[]{:S(2)}, u32[]{:S(2)}) collective-permute-start(f32[8,2,16,256]{3,2,0,1:T(8,128)S(1)} %get-tuple-element.242), channel_id=1, source_target_pairs={{0,1},{1,2},{2,3},{3,4},{4,5},{5,6},{6,7},{8,9},{9,10},{10,11},{11... | collective-permute-start | bytes 786440 | tf_op jit(solution)/shard_map/while/body/eval_jaxpr/ppermute | solution.py:35
  130.7 6.0 %collective-permute-start.1 = (f32[8,2,8,256]{3,2,0,1:T(8,128)}, f32[8,2,8,256]{3,2,0,1:T(8,128)}, u32[]{:S(2)}, u32[]{:S(2)}) collective-permute-start(f32[8,2,8,256]{3,2,0,1:T(8,128)} %get-tuple-element.208), channel_id=1, source_target_pairs={{8,0},{16,8},{24,16},{32,24},{40,32},{48,40},{56,48},{64,56},{72,6... | collective-permute-start | bytes 393224 | tf_op jit(solution)/shard_map/while/body/eval_jaxpr/ppermute | solution.py:25
  151.6 7.6 %collective-permute-start.2 = (f32[8,2,16,256]{3,2,0,1:T(8,128)S(1)}, f32[8,2,16,256]{3,2,0,1:T(8,128)S(1)}, u32[]{:S(2)}, u32[]{:S(2)}) collective-permute-start(f32[8,2,16,256]{3,2,0,1:T(8,128)S(1)} %get-tuple-element.242), channel_id=1, source_target_pairs={{0,1},{1,2},{2,3},{3,4},{4,5},{5,6},{6,7},{8,9},{9,10},{10,11},{11... | collective-permute-start | bytes 786440 | tf_op jit(solution)/shard_map/while/body/eval_jaxpr/ppermute | solution.py:35
  163.0 6.0 %collective-permute-start.1 = (f32[8,2,8,256]{3,2,0,1:T(8,128)}, f32[8,2,8,256]{3,2,0,1:T(8,128)}, u32[]{:S(2)}, u32[]{:S(2)}) collective-permute-start(f32[8,2,8,256]{3,2,0,1:T(8,128)} %get-tuple-element.208), channel_id=1, source_target_pairs={{8,0},{16,8},{24,16},{32,24},{40,32},{48,40},{56,48},{64,56},{72,6... | collective-permute-start | bytes 393224 | tf_op jit(solution)/shard_map/while/body/eval_jaxpr/ppermute | solution.py:25
  183.8 7.6 %collective-permute-start.2 = (f32[8,2,16,256]{3,2,0,1:T(8,128)S(1)}, f32[8,2,16,256]{3,2,0,1:T(8,128)S(1)}, u32[]{:S(2)}, u32[]{:S(2)}) collective-permute-start(f32[8,2,16,256]{3,2,0,1:T(8,128)S(1)} %get-tuple-element.242), channel_id=1, source_target_pairs={{0,1},{1,2},{2,3},{3,4},{4,5},{5,6},{6,7},{8,9},{9,10},{10,11},{11... | collective-permute-start | bytes 786440 | tf_op jit(solution)/shard_map/while/body/eval_jaxpr/ppermute | solution.py:35
  195.2 6.0 %collective-permute-start.1 = (f32[8,2,8,256]{3,2,0,1:T(8,128)}, f32[8,2,8,256]{3,2,0,1:T(8,128)}, u32[]{:S(2)}, u32[]{:S(2)}) collective-permute-start(f32[8,2,8,256]{3,2,0,1:T(8,128)} %get-tuple-element.208), channel_id=1, source_target_pairs={{8,0},{16,8},{24,16},{32,24},{40,32},{48,40},{56,48},{64,56},{72,6... | collective-permute-start | bytes 393224 | tf_op jit(solution)/shard_map/while/body/eval_jaxpr/ppermute | solution.py:25
  216.1 7.6 %collective-permute-start.2 = (f32[8,2,16,256]{3,2,0,1:T(8,128)S(1)}, f32[8,2,16,256]{3,2,0,1:T(8,128)S(1)}, u32[]{:S(2)}, u32[]{:S(2)}) collective-permute-start(f32[8,2,16,256]{3,2,0,1:T(8,128)S(1)} %get-tuple-element.242), channel_id=1, source_target_pairs={{0,1},{1,2},{2,3},{3,4},{4,5},{5,6},{6,7},{8,9},{9,10},{10,11},{11... | collective-permute-start | bytes 786440 | tf_op jit(solution)/shard_map/while/body/eval_jaxpr/ppermute | solution.py:35
  227.5 6.0 %collective-permute-start.1 = (f32[8,2,8,256]{3,2,0,1:T(8,128)}, f32[8,2,8,256]{3,2,0,1:T(8,128)}, u32[]{:S(2)}, u32[]{:S(2)}) collective-permute-start(f32[8,2,8,256]{3,2,0,1:T(8,128)} %get-tuple-element.208), channel_id=1, source_target_pairs={{8,0},{16,8},{24,16},{32,24},{40,32},{48,40},{56,48},{64,56},{72,6... | collective-permute-start | bytes 393224 | tf_op jit(solution)/shard_map/while/body/eval_jaxpr/ppermute | solution.py:25
  248.3 7.6 %collective-permute-start.2 = (f32[8,2,16,256]{3,2,0,1:T(8,128)S(1)}, f32[8,2,16,256]{3,2,0,1:T(8,128)S(1)}, u32[]{:S(2)}, u32[]{:S(2)}) collective-permute-start(f32[8,2,16,256]{3,2,0,1:T(8,128)S(1)} %get-tuple-element.242), channel_id=1, source_target_pairs={{0,1},{1,2},{2,3},{3,4},{4,5},{5,6},{6,7},{8,9},{9,10},{10,11},{11... | collective-permute-start | bytes 786440 | tf_op jit(solution)/shard_map/while/body/eval_jaxpr/ppermute | solution.py:35
  259.7 6.0 %collective-permute-start.1 = (f32[8,2,8,256]{3,2,0,1:T(8,128)}, f32[8,2,8,256]{3,2,0,1:T(8,128)}, u32[]{:S(2)}, u32[]{:S(2)}) collective-permute-start(f32[8,2,8,256]{3,2,0,1:T(8,128)} %get-tuple-element.208), channel_id=1, source_target_pairs={{8,0},{16,8},{24,16},{32,24},{40,32},{48,40},{56,48},{64,56},{72,6... | collective-permute-start | bytes 393224 | tf_op jit(solution)/shard_map/while/body/eval_jaxpr/ppermute | solution.py:25
  280.6 7.8 %collective-permute-start.2 = (f32[8,2,16,256]{3,2,0,1:T(8,128)S(1)}, f32[8,2,16,256]{3,2,0,1:T(8,128)S(1)}, u32[]{:S(2)}, u32[]{:S(2)}) collective-permute-start(f32[8,2,16,256]{3,2,0,1:T(8,128)S(1)} %get-tuple-element.242), channel_id=1, source_target_pairs={{0,1},{1,2},{2,3},{3,4},{4,5},{5,6},{6,7},{8,9},{9,10},{10,11},{11... | collective-permute-start | bytes 786440 | tf_op jit(solution)/shard_map/while/body/eval_jaxpr/ppermute | solution.py:35
  292.3 13.8 %copy.21 = f32[5,8,16,256]{0,2,1,3:T(8,128)} copy(f32[5,8,16,256]{3,0,2,1:T(8,128)S(1)} %fusion.33) | data formatting | bytes 1310720
  306.1 11.9 %reshape.106 = f32[256,640]{1,0:T(8,128)} reshape(f32[256,8,16,5]{3,2,1,0:T(8,128)} %bitcast.201) | data formatting | bytes 1310720
  318.1 43.7 %reduce-scatter.4.cloned.1.call-done = f32[64,640]{1,0:T(8,128)} async-done(((f32[256,640]{1,0:T(8,128)}), f32[64,640]{1,0:T(8,128)}) %reduce-scatter.4.cloned.1.call-update) | async-done | bytes 163856
  361.8 6.2 %reshape.107 = f32[64,8,16,5]{3,2,1,0:T(8,128)} reshape(f32[64,640]{1,0:T(8,128)} %reduce-scatter.4.cloned.1.call-done) | data formatting | bytes 327680
  379.9 8.5 %collective-permute-done.5 = f32[5,8,16,64]{3,0,2,1:T(8,128)S(1)} collective-permute-done((f32[5,8,16,64]{3,0,2,1:T(8,128)S(1)}, f32[5,8,16,64]{3,0,2,1:T(8,128)S(1)}, u32[]{:S(2)}, u32[]{:S(2)}) %collective-permute-start.5) | collective-permute-done | bytes 163872 | tf_op jit(solution)/shard_map/ppermute | solution.py:129
  391.9 11.2 %collective-permute-done.6 = f32[5,8,16,64]{3,0,2,1:T(8,128)} collective-permute-done((f32[5,8,16,64]{3,0,2,1:T(8,128)S(1)}, f32[5,8,16,64]{3,0,2,1:T(8,128)}, u32[]{:S(2)}, u32[]{:S(2)}) %collective-permute-start.6) | collective-permute-done | bytes 163872 | tf_op jit(solution)/shard_map/ppermute | solution.py:129
  (653 shorter events, 186.0 us)
Async XLA Ops:
  7.2 354.7 %reduce-scatter.4.cloned.1.call-start = ((), (), s32[]{:S(2)}) async-start(), calls=%async_computation.1 | async-start | bytes 819200
  8.7 21.3 %collective-permute-start.3 = (f32[7,8,8,256]{3,2,1,0:T(8,128)S(1)}, f32[7,8,8,256]{3,2,1,0:T(8,128)S(1)}, u32[]{:S(2)}, u32[]{:S(2)}) collective-permute-start(f32[7,8,8,256]{3,2,1,0:T(8,128)S(1)} %get-tuple-element.112), channel_id=1, source_target_pairs={{0,8},{8,16},{16,24},{24,32},{32,40},{40,48},{48,56},{56,64},{64,7... | collective-permute-start | bytes 1376264 | tf_op jit(solution)/shard_map/ppermute | solution.py:23
  13.0 18.2 %collective-permute-start.4 = (f32[7,8,8,256]{3,2,1,0:T(8,128)S(1)}, f32[7,8,8,256]{3,2,1,0:T(8,128)}, u32[]{:S(2)}, u32[]{:S(2)}) collective-permute-start(f32[7,8,8,256]{3,2,1,0:T(8,128)S(1)} %get-tuple-element.113), channel_id=1, source_target_pairs={{8,0},{16,8},{24,16},{32,24},{40,32},{48,40},{56,48},{64,56},{72,6... | collective-permute-start | bytes 1376264 | tf_op jit(solution)/shard_map/ppermute | solution.py:25
  38.6 13.2 %collective-permute-start = (f32[8,2,8,256]{3,2,0,1:T(8,128)}, f32[8,2,8,256]{3,2,0,1:T(8,128)}, u32[]{:S(2)}, u32[]{:S(2)}) collective-permute-start(f32[8,2,8,256]{3,2,0,1:T(8,128)} %get-tuple-element.207), channel_id=1, source_target_pairs={{0,8},{8,16},{16,24},{24,32},{32,40},{40,48},{48,56},{56,64},{64,7... | collective-permute-start | bytes 393224 | tf_op jit(solution)/shard_map/while/body/eval_jaxpr/ppermute | solution.py:23
  40.5 13.2 %collective-permute-start.1 = (f32[8,2,8,256]{3,2,0,1:T(8,128)}, f32[8,2,8,256]{3,2,0,1:T(8,128)}, u32[]{:S(2)}, u32[]{:S(2)}) collective-permute-start(f32[8,2,8,256]{3,2,0,1:T(8,128)} %get-tuple-element.208), channel_id=1, source_target_pairs={{8,0},{16,8},{24,16},{32,24},{40,32},{48,40},{56,48},{64,56},{72,6... | collective-permute-start | bytes 393224 | tf_op jit(solution)/shard_map/while/body/eval_jaxpr/ppermute | solution.py:25
  65.1 12.6 %collective-permute-start = (f32[8,2,8,256]{3,2,0,1:T(8,128)}, f32[8,2,8,256]{3,2,0,1:T(8,128)}, u32[]{:S(2)}, u32[]{:S(2)}) collective-permute-start(f32[8,2,8,256]{3,2,0,1:T(8,128)} %get-tuple-element.207), channel_id=1, source_target_pairs={{0,8},{8,16},{16,24},{24,32},{32,40},{40,48},{48,56},{56,64},{64,7... | collective-permute-start | bytes 393224 | tf_op jit(solution)/shard_map/while/body/eval_jaxpr/ppermute | solution.py:23
  67.1 12.6 %collective-permute-start.1 = (f32[8,2,8,256]{3,2,0,1:T(8,128)}, f32[8,2,8,256]{3,2,0,1:T(8,128)}, u32[]{:S(2)}, u32[]{:S(2)}) collective-permute-start(f32[8,2,8,256]{3,2,0,1:T(8,128)} %get-tuple-element.208), channel_id=1, source_target_pairs={{8,0},{16,8},{24,16},{32,24},{40,32},{48,40},{56,48},{64,56},{72,6... | collective-permute-start | bytes 393224 | tf_op jit(solution)/shard_map/while/body/eval_jaxpr/ppermute | solution.py:25
  96.6 12.6 %collective-permute-start = (f32[8,2,8,256]{3,2,0,1:T(8,128)}, f32[8,2,8,256]{3,2,0,1:T(8,128)}, u32[]{:S(2)}, u32[]{:S(2)}) collective-permute-start(f32[8,2,8,256]{3,2,0,1:T(8,128)} %get-tuple-element.207), channel_id=1, source_target_pairs={{0,8},{8,16},{16,24},{24,32},{32,40},{40,48},{48,56},{56,64},{64,7... | collective-permute-start | bytes 393224 | tf_op jit(solution)/shard_map/while/body/eval_jaxpr/ppermute | solution.py:23
  98.6 12.6 %collective-permute-start.1 = (f32[8,2,8,256]{3,2,0,1:T(8,128)}, f32[8,2,8,256]{3,2,0,1:T(8,128)}, u32[]{:S(2)}, u32[]{:S(2)}) collective-permute-start(f32[8,2,8,256]{3,2,0,1:T(8,128)} %get-tuple-element.208), channel_id=1, source_target_pairs={{8,0},{16,8},{24,16},{32,24},{40,32},{48,40},{56,48},{64,56},{72,6... | collective-permute-start | bytes 393224 | tf_op jit(solution)/shard_map/while/body/eval_jaxpr/ppermute | solution.py:25
  128.8 12.6 %collective-permute-start = (f32[8,2,8,256]{3,2,0,1:T(8,128)}, f32[8,2,8,256]{3,2,0,1:T(8,128)}, u32[]{:S(2)}, u32[]{:S(2)}) collective-permute-start(f32[8,2,8,256]{3,2,0,1:T(8,128)} %get-tuple-element.207), channel_id=1, source_target_pairs={{0,8},{8,16},{16,24},{24,32},{32,40},{40,48},{48,56},{56,64},{64,7... | collective-permute-start | bytes 393224 | tf_op jit(solution)/shard_map/while/body/eval_jaxpr/ppermute | solution.py:23
  130.7 12.6 %collective-permute-start.1 = (f32[8,2,8,256]{3,2,0,1:T(8,128)}, f32[8,2,8,256]{3,2,0,1:T(8,128)}, u32[]{:S(2)}, u32[]{:S(2)}) collective-permute-start(f32[8,2,8,256]{3,2,0,1:T(8,128)} %get-tuple-element.208), channel_id=1, source_target_pairs={{8,0},{16,8},{24,16},{32,24},{40,32},{48,40},{56,48},{64,56},{72,6... | collective-permute-start | bytes 393224 | tf_op jit(solution)/shard_map/while/body/eval_jaxpr/ppermute | solution.py:25
  151.6 8.7 %collective-permute-start.2 = (f32[8,2,16,256]{3,2,0,1:T(8,128)S(1)}, f32[8,2,16,256]{3,2,0,1:T(8,128)S(1)}, u32[]{:S(2)}, u32[]{:S(2)}) collective-permute-start(f32[8,2,16,256]{3,2,0,1:T(8,128)S(1)} %get-tuple-element.242), channel_id=1, source_target_pairs={{0,1},{1,2},{2,3},{3,4},{4,5},{5,6},{6,7},{8,9},{9,10},{10,11},{11... | collective-permute-start | bytes 786440 | tf_op jit(solution)/shard_map/while/body/eval_jaxpr/ppermute | solution.py:35
  161.1 12.6 %collective-permute-start = (f32[8,2,8,256]{3,2,0,1:T(8,128)}, f32[8,2,8,256]{3,2,0,1:T(8,128)}, u32[]{:S(2)}, u32[]{:S(2)}) collective-permute-start(f32[8,2,8,256]{3,2,0,1:T(8,128)} %get-tuple-element.207), channel_id=1, source_target_pairs={{0,8},{8,16},{16,24},{24,32},{32,40},{40,48},{48,56},{56,64},{64,7... | collective-permute-start | bytes 393224 | tf_op jit(solution)/shard_map/while/body/eval_jaxpr/ppermute | solution.py:23
  163.0 12.6 %collective-permute-start.1 = (f32[8,2,8,256]{3,2,0,1:T(8,128)}, f32[8,2,8,256]{3,2,0,1:T(8,128)}, u32[]{:S(2)}, u32[]{:S(2)}) collective-permute-start(f32[8,2,8,256]{3,2,0,1:T(8,128)} %get-tuple-element.208), channel_id=1, source_target_pairs={{8,0},{16,8},{24,16},{32,24},{40,32},{48,40},{56,48},{64,56},{72,6... | collective-permute-start | bytes 393224 | tf_op jit(solution)/shard_map/while/body/eval_jaxpr/ppermute | solution.py:25
  193.3 12.6 %collective-permute-start = (f32[8,2,8,256]{3,2,0,1:T(8,128)}, f32[8,2,8,256]{3,2,0,1:T(8,128)}, u32[]{:S(2)}, u32[]{:S(2)}) collective-permute-start(f32[8,2,8,256]{3,2,0,1:T(8,128)} %get-tuple-element.207), channel_id=1, source_target_pairs={{0,8},{8,16},{16,24},{24,32},{32,40},{40,48},{48,56},{56,64},{64,7... | collective-permute-start | bytes 393224 | tf_op jit(solution)/shard_map/while/body/eval_jaxpr/ppermute | solution.py:23
  195.2 12.6 %collective-permute-start.1 = (f32[8,2,8,256]{3,2,0,1:T(8,128)}, f32[8,2,8,256]{3,2,0,1:T(8,128)}, u32[]{:S(2)}, u32[]{:S(2)}) collective-permute-start(f32[8,2,8,256]{3,2,0,1:T(8,128)} %get-tuple-element.208), channel_id=1, source_target_pairs={{8,0},{16,8},{24,16},{32,24},{40,32},{48,40},{56,48},{64,56},{72,6... | collective-permute-start | bytes 393224 | tf_op jit(solution)/shard_map/while/body/eval_jaxpr/ppermute | solution.py:25
  225.6 12.6 %collective-permute-start = (f32[8,2,8,256]{3,2,0,1:T(8,128)}, f32[8,2,8,256]{3,2,0,1:T(8,128)}, u32[]{:S(2)}, u32[]{:S(2)}) collective-permute-start(f32[8,2,8,256]{3,2,0,1:T(8,128)} %get-tuple-element.207), channel_id=1, source_target_pairs={{0,8},{8,16},{16,24},{24,32},{32,40},{40,48},{48,56},{56,64},{64,7... | collective-permute-start | bytes 393224 | tf_op jit(solution)/shard_map/while/body/eval_jaxpr/ppermute | solution.py:23
  227.5 12.6 %collective-permute-start.1 = (f32[8,2,8,256]{3,2,0,1:T(8,128)}, f32[8,2,8,256]{3,2,0,1:T(8,128)}, u32[]{:S(2)}, u32[]{:S(2)}) collective-permute-start(f32[8,2,8,256]{3,2,0,1:T(8,128)} %get-tuple-element.208), channel_id=1, source_target_pairs={{8,0},{16,8},{24,16},{32,24},{40,32},{48,40},{56,48},{64,56},{72,6... | collective-permute-start | bytes 393224 | tf_op jit(solution)/shard_map/while/body/eval_jaxpr/ppermute | solution.py:25
  257.8 12.6 %collective-permute-start = (f32[8,2,8,256]{3,2,0,1:T(8,128)}, f32[8,2,8,256]{3,2,0,1:T(8,128)}, u32[]{:S(2)}, u32[]{:S(2)}) collective-permute-start(f32[8,2,8,256]{3,2,0,1:T(8,128)} %get-tuple-element.207), channel_id=1, source_target_pairs={{0,8},{8,16},{16,24},{24,32},{32,40},{40,48},{48,56},{56,64},{64,7... | collective-permute-start | bytes 393224 | tf_op jit(solution)/shard_map/while/body/eval_jaxpr/ppermute | solution.py:23
  259.7 12.6 %collective-permute-start.1 = (f32[8,2,8,256]{3,2,0,1:T(8,128)}, f32[8,2,8,256]{3,2,0,1:T(8,128)}, u32[]{:S(2)}, u32[]{:S(2)}) collective-permute-start(f32[8,2,8,256]{3,2,0,1:T(8,128)} %get-tuple-element.208), channel_id=1, source_target_pairs={{8,0},{16,8},{24,16},{32,24},{40,32},{48,40},{56,48},{64,56},{72,6... | collective-permute-start | bytes 393224 | tf_op jit(solution)/shard_map/while/body/eval_jaxpr/ppermute | solution.py:25
  280.6 9.0 %collective-permute-start.2 = (f32[8,2,16,256]{3,2,0,1:T(8,128)S(1)}, f32[8,2,16,256]{3,2,0,1:T(8,128)S(1)}, u32[]{:S(2)}, u32[]{:S(2)}) collective-permute-start(f32[8,2,16,256]{3,2,0,1:T(8,128)S(1)} %get-tuple-element.242), channel_id=1, source_target_pairs={{0,1},{1,2},{2,3},{3,4},{4,5},{5,6},{6,7},{8,9},{9,10},{10,11},{11... | collective-permute-start | bytes 786440 | tf_op jit(solution)/shard_map/while/body/eval_jaxpr/ppermute | solution.py:35
  372.8 15.6 %collective-permute-start.5 = (f32[5,8,16,64]{3,0,2,1:T(8,128)S(1)}, f32[5,8,16,64]{3,0,2,1:T(8,128)S(1)}, u32[]{:S(2)}, u32[]{:S(2)}) collective-permute-start(f32[5,8,16,64]{3,0,2,1:T(8,128)S(1)} %maximum_divide_fusion), channel_id=1, source_target_pairs={{0,128},{128,256},{256,384},{384,0},{1,129},{129,257},{257,385},{3... | collective-permute-start | bytes 491528 | tf_op jit(solution)/shard_map/ppermute | solution.py:129
  374.8 16.3 %collective-permute-start.7 = (f32[5,8,16,64]{3,0,2,1:T(8,128)S(1)}, f32[5,8,16,64]{3,0,2,1:T(8,128)S(1)}, u32[]{:S(2)}, u32[]{:S(2)}) collective-permute-start(f32[5,8,16,64]{3,0,2,1:T(8,128)S(1)} %maximum_divide_fusion), channel_id=1, source_target_pairs={{0,384},{128,0},{256,128},{384,256},{1,385},{129,1},{257,129},{385... | collective-permute-start | bytes 491528 | tf_op jit(solution)/shard_map/ppermute | solution.py:131
  388.4 14.7 %collective-permute-start.6 = (f32[5,8,16,64]{3,0,2,1:T(8,128)S(1)}, f32[5,8,16,64]{3,0,2,1:T(8,128)}, u32[]{:S(2)}, u32[]{:S(2)}) collective-permute-start(f32[5,8,16,64]{3,0,2,1:T(8,128)S(1)} %collective-permute-done.5), channel_id=1, source_target_pairs={{0,128},{128,256},{256,384},{384,0},{1,129},{129,257},{257,385},{3... | collective-permute-start | bytes 491528 | tf_op jit(solution)/shard_map/ppermute | solution.py:129
  (79 other events, 629.5 us)
Sparse Core Ops, SparseCore 0:
  318.1 43.6 reduce-scatter.3
